TPU v7x, 32 devices: a whole 2x2x4 slice. The times are simulated.
32 devices in a mesh: dp: 4 (over z), expert: 2 (over x), tensor: 4 (over y, core).
Axes of the slice: x: 2, y: 2, z: 4, core: 2. Of those that a mesh axis runs over, the one named last changes fastest.
Arguments:
- tokens: bfloat16 [128, 4096], P(('dp', 'expert', 'tensor')), may hold values from -6 to 6
- routes: int32 [128, 2], P(('dp', 'expert', 'tensor')), may hold values from 0 to 7, all different within a row; in each aligned block of 4 rows (0 to 3, 4 to 7, ...) at most 2 rows name the same one
- gates: float32 [128, 2], P(('dp', 'expert', 'tensor')), may hold values from 0.1 to 1
- d_out: bfloat16 [128, 4096], P(('dp', 'expert', 'tensor')), may hold values from -3 to 3
- w_in: bfloat16 [8, 2, 7168, 4096], P('expert', None, ('dp', 'tensor')), may hold values from -0.09375 to 0.09375
- w_out: bfloat16 [8, 7168, 4096], P('expert', ('dp', 'tensor')), may hold values from -0.0625 to 0.0625
Outputs:
- mixed: bfloat16 [128, 4096], P(('dp', 'expert', 'tensor'))
- d_tokens: bfloat16 [128, 4096], P(('dp', 'expert', 'tensor'))
- d_gates: float32 [128, 2], P(('dp', 'expert', 'tensor'))
- grad_in: bfloat16 [8, 2, 7168, 4096], P('expert', None, ('dp', 'tensor'))
- grad_out: bfloat16 [8, 7168, 4096], P('expert', ('dp', 'tensor'))
Inputs may be any that keep to these rules, and one draw needn't show every extreme that they name: `routes`: each token names 2 different experts; among the 4 tokens of one device no expert is named more than 2 times, a bound that some block reaches.
All inputs are finite; a program needn't handle non-finite values.
Results may differ from a plain program's by a relative error of at most 0.0065.
Values may be sent and summed in bfloat16 or wider, within the bound.
No kernel may reach another device: no remote copies, remote signals or barrier semaphores. Data moves between devices by JAX's collectives and lax.ppermute only.
A program may use at most 192 MiB of HBM per device.

v0:
```python
import jax
import jax.numpy as jnp
from jax import lax
from jax.sharding import PartitionSpec as P

CAP = 2


def to_groups(buffer, owners, local_experts):
    width = buffer.shape[-1]
    shaped = buffer.reshape(owners, local_experts, CAP, width)
    return jnp.swapaxes(shaped, 0, 1).reshape(local_experts, owners * CAP, width)


def to_owners(summed, owners, local_experts):
    width = summed.shape[-1]
    shaped = summed.astype(jnp.bfloat16).reshape(local_experts, owners, CAP, width)
    return jnp.swapaxes(shaped, 0, 1).reshape(owners, local_experts * CAP, width)


def per_device(tokens, routes, gates, d_out, w_in, w_out):
    tok_count, width = tokens.shape
    top_k = routes.shape[1]
    owners = lax.axis_size("expert")
    local_experts = w_in.shape[0]
    experts_all = owners * local_experts
    flat_routes = routes.reshape(-1)
    one_hot = (flat_routes[:, None] == jnp.arange(experts_all, dtype=jnp.int32)[None, :]).astype(
        jnp.int32
    )
    earlier = jnp.cumsum(one_hot, axis=0) - one_hot
    slot_index = jnp.sum(earlier * one_hot, axis=1)
    target = flat_routes * CAP + slot_index
    placement = (jnp.arange(experts_all * CAP, dtype=jnp.int32)[:, None] == target[None, :]).astype(
        jnp.bfloat16
    )
    token_rows = jnp.repeat(tokens, top_k, axis=0)
    scaled = (gates.reshape(-1, 1) * jnp.repeat(d_out, top_k, axis=0).astype(jnp.float32)).astype(
        jnp.bfloat16
    )
    send_x = jnp.dot(placement, token_rows, preferred_element_type=jnp.float32).astype(jnp.bfloat16)
    send_g = jnp.dot(placement, scaled, preferred_element_type=jnp.float32).astype(jnp.bfloat16)
    send_x = send_x.reshape(owners, local_experts * CAP, width)
    send_g = send_g.reshape(owners, local_experts * CAP, width)
    got_x, got_g = (
        lax.all_to_all(send_x, "expert", split_axis=0, concat_axis=0, tiled=True),
        lax.all_to_all(send_g, "expert", split_axis=0, concat_axis=0, tiled=True),
    )
    rows_x, rows_g = (
        lax.all_gather(
            to_groups(got_x, owners, local_experts), ("dp", "tensor"), axis=1, tiled=True
        ),
        lax.all_gather(
            to_groups(got_g, owners, local_experts), ("dp", "tensor"), axis=1, tiled=True
        ),
    )
    both_pre = jnp.einsum("lrd,lkfd->lkrf", rows_x, w_in, preferred_element_type=jnp.float32)
    gate_pre = both_pre[:, 0]
    up_pre = both_pre[:, 1]
    sigma = jax.nn.sigmoid(gate_pre)
    hidden = (gate_pre * sigma * up_pre).astype(jnp.bfloat16)
    out_terms = jnp.einsum("lrf,lfd->lrd", hidden, w_out, preferred_element_type=jnp.float32)
    out_sum = lax.psum_scatter(out_terms, ("dp", "tensor"), scatter_dimension=1, tiled=True)
    out_back = lax.all_to_all(
        to_owners(out_sum, owners, local_experts), "expert", split_axis=0, concat_axis=0, tiled=True
    )
    d_hidden = jnp.einsum("lrd,lfd->lrf", rows_g, w_out, preferred_element_type=jnp.float32)
    d_gate = d_hidden * up_pre * sigma * (1.0 + gate_pre * (1.0 - sigma))
    d_up = d_hidden * gate_pre * sigma
    d_pre = jnp.stack([d_gate, d_up], axis=1).astype(jnp.bfloat16)
    dx_terms = jnp.einsum("lkrf,lkfd->lrd", d_pre, w_in, preferred_element_type=jnp.float32)
    grad_out = jnp.einsum(
        "lrf,lrd->lfd", hidden, rows_g, preferred_element_type=jnp.float32
    ).astype(jnp.bfloat16)
    grad_in = jnp.einsum(
        "lkrf,lrd->lkfd", d_pre, rows_x, preferred_element_type=jnp.float32
    ).astype(jnp.bfloat16)
    dx_sum = lax.psum_scatter(dx_terms, ("dp", "tensor"), scatter_dimension=1, tiled=True)
    dx_back = lax.all_to_all(
        to_owners(dx_sum, owners, local_experts), "expert", split_axis=0, concat_axis=0, tiled=True
    )
    out_buffer = out_back.reshape(experts_all * CAP, width)
    dx_buffer = dx_back.reshape(experts_all * CAP, width)
    out_route = jnp.einsum(
        "pj,pd->jd", placement, out_buffer, preferred_element_type=jnp.float32
    ).reshape(tok_count, top_k, width)
    dx_route = jnp.einsum(
        "pj,pd->jd", placement, dx_buffer, preferred_element_type=jnp.float32
    ).reshape(tok_count, top_k, width)
    mixed = jnp.sum(gates[:, :, None] * out_route, axis=1).astype(jnp.bfloat16)
    d_tokens = jnp.sum(dx_route, axis=1).astype(jnp.bfloat16)
    d_gates = jnp.sum(d_out.astype(jnp.float32)[:, None, :] * out_route, axis=2)
    return (mixed, d_tokens, d_gates, grad_in, grad_out)


def solution(mesh):
    return jax.shard_map(
        per_device,
        mesh=mesh,
        in_specs=(
            P(("dp", "expert", "tensor"), None),
            P(("dp", "expert", "tensor"), None),
            P(("dp", "expert", "tensor"), None),
            P(("dp", "expert", "tensor"), None),
            P("expert", None, ("dp", "tensor"), None),
            P("expert", ("dp", "tensor"), None),
        ),
        out_specs=(
            P(("dp", "expert", "tensor"), None),
            P(("dp", "expert", "tensor"), None),
            P(("dp", "expert", "tensor"), None),
            P("expert", None, ("dp", "tensor"), None),
            P("expert", ("dp", "tensor"), None),
        ),
        check_vma=False,
    )
```

profile of v0, /device:TPU:1, one launch (start us, length us, event | category | flops | bytes accessed | tf_op | source)
XLA Modules:
  0.0 361.7 jit_solution(2922438015457980727)
XLA Ops:
  7.2 0.8 copy.52
  8.2 0.2 select_reduce_fusion
  8.4 0.8 broadcast_in_dim.4
  9.2 0.2 fusion.5
  9.4 6.4 %all_to_all.20 = bf16[2,8,4096]{2,1,0:T(8,128)(2,1)S(1)} all-to-all(bf16[2,8,4096]{2,1,0:T(8,128)(2,1)S(1)} %fusion.5), channel_id=1, replica_groups=mesh['dp'=4,'expert'=2,'tensor'=4] {'expert'}, dimensions={0} | all-to-all | bytes 262144 | tf_op jit(solution)/shard_map/all_to_all | solution.py:46
  15.9 0.8 copy.53
  16.7 0.8 broadcast_in_dim.5.clone
  17.6 0.8 copy.59
  18.5 0.2 fusion.6
  18.7 5.7 %all_to_all.21 = bf16[2,8,4096]{2,1,0:T(8,128)(2,1)S(1)} all-to-all(bf16[2,8,4096]{2,1,0:T(8,128)(2,1)S(1)} %fusion.6), channel_id=1, replica_groups=mesh['dp'=4,'expert'=2,'tensor'=4] {'expert'}, dimensions={0} | all-to-all | bytes 262144 | tf_op jit(solution)/shard_map/all_to_all | solution.py:47
  24.5 0.8 copy.61
  25.3 0.8 convert_element_type.48
  26.2 1.2 dynamic-slice
  28.1 32.3 %all-gather.3.cloned.1.call-done = bf16[4,64,4096]{2,0,1:T(4,128)(2,1)} async-done(((bf16[4,4,4096]{2,0,1:T(4,128)(2,1)}), bf16[4,64,4096]{2,0,1:T(4,128)(2,1)}) %all-gather.3.cloned.1.call-update) | async-done | bytes 2097168 | tf_op jit(solution)/shard_map/all_gather | solution.py:50
  60.4 14.6 %fusion.13 = f32[4,2,64,448]{3,2,1,0:T(8,128)S(1)} fusion(bf16[4,2,448,4096]{3,2,1,0:T(8,128)(2,1)} %param.10, bf16[4,64,4096,1]{2,0,1,3:T(4,128)(2,1)} %bitcast.71), kind=kOutput, calls=%fused_computation.15 | convolution fusion | flops 1879048192 | bytes 32374784 | tf_op jit(solution)/shard_map/lrd,lkfd->lkrf/dot_general | solution.py:57
  75.0 28.4 %all-gather.5.cloned.1.call-done = bf16[4,64,4096]{2,0,1:T(4,128)(2,1)} async-done(((bf16[4,4,4096]{2,0,1:T(4,128)(2,1)}), bf16[4,64,4096]{2,0,1:T(4,128)(2,1)}) %all-gather.5.cloned.1.call-update) | async-done | bytes 2097168 | tf_op jit(solution)/shard_map/all_gather | solution.py:53
  103.4 10.4 %fusion.18 = (bf16[4,1,64,448]{3,2,0,1:T(8,128)(2,1)S(1)}, bf16[4,1,64,448]{3,2,0,1:T(8,128)(2,1)S(1)}, bf16[4,64,448]{2,1,0:T(8,128)(2,1)S(1)}) fusion(f32[4,2,64,448]{3,2,1,0:T(8,128)S(1)} %fusion.13, bf16[4,448,4096]{2,1,0:T(8,128)(2,1)} %param.11, bf16[4,64,4096]{2,0,1:T(4,128)(2,1)} %all-gather.5.cloned.1.call-done), kind=kOutput, calls=%fused_computation.28 | convolution fusion | flops 941359104 | bytes 18382848 | tf_op jit(solution)/shard_map/lrd,lfd->lrf/dot_general | solution.py:67
  113.7 14.2 %fusion.2 = f32[4,64,4096]{2,1,0:T(8,128)} fusion(bf16[4,2,448,4096]{3,2,1,0:T(8,128)(2,1)} %param.10, bf16[4,1,64,448]{3,2,0,1:T(8,128)(2,1)S(1)} %get-tuple-element.10, bf16[4,1,64,448]{3,2,0,1:T(8,128)(2,1)S(1)} %get-tuple-element.9), kind=kOutput, calls=%fused_computation.4 | convolution fusion | flops 1879277568 | bytes 34013184 | tf_op jit(solution)/shard_map/lkrf,lkfd->lrd/dot_general | solution.py:71
  128.0 12.8 %convolution_convert_fusion = bf16[4,2,448,4096]{3,2,1,0:T(8,128)(2,1)} fusion(bf16[4,64,4096,1]{2,0,1,3:T(4,128)(2,1)S(1)} %bitcast.72, bf16[4,1,64,448]{3,2,0,1:T(8,128)(2,1)S(1)} %get-tuple-element.10, bf16[4,1,64,448]{3,2,0,1:T(8,128)(2,1)S(1)} %get-tuple-element.9), kind=kOutput, calls=%fused_computation.2 | convolution fusion | flops 1893957632 | bytes 31916032 | tf_op jit(solution)/shard_map/lkrf,lrd->lkfd/dot_general | solution.py:75
  140.8 9.8 %fusion.30 = f32[4,64,4096]{2,1,0:T(8,128)} fusion(bf16[4,64,448]{2,1,0:T(8,128)(2,1)S(1)} %get-tuple-element.11, bf16[4,448,4096]{2,1,0:T(8,128)(2,1)} %param.11), kind=kOutput, calls=%fused_computation.46 | convolution fusion | flops 939524096 | bytes 19103744 | tf_op jit(solution)/shard_map/lrf,lfd->lrd/dot_general | solution.py:62
  150.6 182.6 %all-reduce.4 = (bf16[4,64,4096]{2,1,0:T(8,128)(2,1)}, bf16[4,64,4096]{2,1,0:T(8,128)(2,1)}) all-reduce(f32[4,64,4096]{2,1,0:T(8,128)} %fusion.30, f32[4,64,4096]{2,1,0:T(8,128)} %fusion.2), channel_id=2, replica_groups=mesh['dp'=4,'expert'=2,'tensor'=4] {'dp','tensor'}, use_global_device_ids=true, to_apply=%region_2.3.clone | all-reduce | flops 2097152 | bytes 12582912
  333.2 1.2 dynamic-slice_convert_fusion
  334.4 0.1 copy.64
  334.6 0.7 copy.65
  335.3 3.4 all-to-all-start.3
  338.7 7.6 %convolution_convert_fusion.1 = bf16[4,448,4096]{2,1,0:T(8,128)(2,1)} fusion(bf16[4,64,448]{2,1,0:T(8,128)(2,1)S(1)} %get-tuple-element.11, bf16[4,64,4096]{2,0,1:T(4,128)(2,1)S(1)} %copy-done), kind=kOutput, calls=%fused_computation.3 | convolution fusion | flops 946864128 | bytes 17006592 | tf_op jit(solution)/shard_map/lrf,lrd->lfd/dot_general | solution.py:72
  346.4 0.1 copy.56
  346.5 0.7 copy.57
  347.3 3.4 all-to-all-start.1
  350.7 0.8 convolution_reduce_fusion
  351.5 2.5 all-to-all-done.1
  354.0 0.9 multiply_reduce_fusion
  (24 shorter events, 1.0 us)
Async XLA Ops:
  7.2 53.2 %all-gather.3.cloned.1.call-start = ((), (), s32[]{:S(2)}) async-start(), calls=%async_computation.4 | async-start | bytes 2228224 | tf_op jit(solution)/shard_map/all_gather | solution.py:50
  16.7 86.7 %all-gather.5.cloned.1.call-start = ((), (), s32[]{:S(2)}) async-start(), calls=%async_computation.5 | async-start | bytes 2228224 | tf_op jit(solution)/shard_map/all_gather | solution.py:53
  113.7 14.3 %copy-start.1 = (bf16[4,64,4096]{2,0,1:T(4,128)(2,1)S(1)}, bf16[4,64,4096]{2,0,1:T(4,128)(2,1)}, u32[]{:S(2)}) copy-start(bf16[4,64,4096]{2,0,1:T(4,128)(2,1)} %all-gather.3.cloned.1.call-done) | copy-start | bytes 6291460
  150.6 188.1 %copy-start = (bf16[4,64,4096]{2,0,1:T(4,128)(2,1)S(1)}, bf16[4,64,4096]{2,0,1:T(4,128)(2,1)}, u32[]{:S(2)}) copy-start(bf16[4,64,4096]{2,0,1:T(4,128)(2,1)} %all-gather.5.cloned.1.call-done) | copy-start | bytes 6291460
  335.3 12.0 %all-to-all-start.3 = ((bf16[2,8,4096]{2,1,0:T(8,128)(2,1)}), bf16[2,8,4096]{2,1,0:T(8,128)(2,1)S(1)}, u32[]{:S(2)}, u32[]{:S(2)}) async-start(bf16[2,8,4096]{2,1,0:T(8,128)(2,1)} %copy.65), calls=%async_computation.3 | async-start | bytes 262144 | tf_op jit(solution)/shard_map/all_to_all | solution.py:79
  338.7 15.3 %copy-start.2 = (f32[4,2]{0,1:T(2,128)S(1)}, f32[4,2]{0,1:T(2,128)}, u32[]{:S(2)}) copy-start(f32[4,2]{0,1:T(2,128)} %param.8) | copy-start | bytes 100
  347.3 6.7 %all-to-all-start.1 = ((bf16[2,8,4096]{2,1,0:T(8,128)(2,1)}), bf16[2,8,4096]{2,1,0:T(8,128)(2,1)S(1)}, u32[]{:S(2)}, u32[]{:S(2)}) async-start(bf16[2,8,4096]{2,1,0:T(8,128)(2,1)} %copy.57), calls=%async_computation.1 | async-start | bytes 262144 | tf_op jit(solution)/shard_map/all_to_all | solution.py:64
Sparse Core Ops, SparseCore 0:
  16.8 43.5 all-gather.2
  63.1 40.1 all-gather.4
where the time goes:
time: 362 us
  blocking collectives  195 us (54%)
  matrix products  71.5 us (20%)
  waiting for transfers between devices  63.3 us (17%)
  between operations  14.8 us (4%)
  local copies, waits for them, and re-layouts  9.46 us (3%)
  starting transfers between devices  6.83 us (2%)
    unnamed x1, blocking collectives  183 us
    all_gather x1, waiting for transfers between devices, per_device(): lax.all_gather(to_groups(got_x, owners, local_experts), ('dp', 'tensor'),...  32.3 us
    all_gather x1, waiting for transfers between devices, per_device(): lax.all_gather(to_groups(got_g, owners, local_experts), ('dp', 'tensor'),...  28.4 us
    dot_general x1, matrix products, per_device(): jnp.einsum('lrd,lkfd->lkrf', rows_x, w_in, preferred_element_type=jnp.flo...  14.6 us
    dot_general x1, matrix products, per_device(): jnp.einsum('lkrf,lkfd->lrd', d_pre, w_in, preferred_element_type=jnp.floa...  14.2 us
    dot_general x1, matrix products, per_device(): jnp.einsum('lkrf,lrd->lkfd', d_pre, rows_x, preferred_element_type=jnp.fl...  12.8 us
    dot_general x1, matrix products, per_device(): jnp.einsum('lrd,lfd->lrf', rows_g, w_out, preferred_element_type=jnp.floa...  10.4 us
    dot_general x1, matrix products, per_device(): jnp.einsum('lrf,lfd->lrd', hidden, w_out, preferred_element_type=jnp.floa...  9.81 us
  transfers between devices with their start and end apart: 4, of which 3 were waited for; matrix products, arithmetic and copies ran while one was open for 8% of the time, Pallas kernels for 0%

commit v1 on v0

v1 whole, which is shorter than its diff:
```python
import jax
import jax.numpy as jnp
from jax import lax
from jax.sharding import PartitionSpec as P

ALL = ("dp", "expert", "tensor")


def dot(a, b, dims):
    return lax.dot_general(a, b, (dims, ((), ())), preferred_element_type=jnp.float32)


def split3(v):
    top = lax.reduce_precision(v, 8, 7)
    mid = lax.reduce_precision(v - top, 8, 7)
    return [top, mid, v - top - mid]


def spread(v, axis):
    copies = jnp.broadcast_to(v[None], (lax.axis_size(axis),) + v.shape)
    return lax.all_to_all(copies, axis, split_axis=0, concat_axis=0, tiled=True)


def per_device(tokens, routes, gates, d_out, w_in, w_out):
    tok_count, width = tokens.shape
    top_k = routes.shape[1]
    local_experts, _, ff, _ = w_in.shape
    n = lax.axis_size(ALL)
    first = lax.axis_index("expert") * local_experts
    small = jnp.concatenate([routes.astype(jnp.float32)] + split3(gates), axis=1)
    small = jnp.pad(small, ((0, 0), (0, 128 - small.shape[1]))).astype(jnp.bfloat16)
    sent = jnp.concatenate([tokens, d_out, small], axis=1)
    for axis in ALL:
        sent = spread(sent, axis)
    sent = sent.reshape(n * tok_count, -1)
    x = sent[:, :width]
    g = sent[:, width : 2 * width]
    extra = sent[:, 2 * width :].astype(jnp.float32)
    routes_all = extra[:, :top_k].astype(jnp.int32)
    gates_all = (
        extra[:, top_k : 2 * top_k] + extra[:, 2 * top_k : 3 * top_k] + extra[:, 3 * top_k : 4 * top_k]
    )
    names = first + jnp.arange(local_experts, dtype=jnp.int32)
    hit = (routes_all[:, :, None] == names[None, None, :]).astype(jnp.float32)
    gate = jnp.sum(gates_all[:, :, None] * hit, axis=1)
    rows = n * tok_count
    w_both = w_in.reshape(local_experts * 2 * ff, width)
    w_down = w_out.reshape(local_experts * ff, width)
    pre = dot(x, w_both, ((1,), (1,))).reshape(rows, local_experts, 2, ff)
    d_raw = dot(g, w_down, ((1,), (1,))).reshape(rows, local_experts, ff)
    gate_pre = pre[:, :, 0]
    up_pre = pre[:, :, 1]
    sigma = jax.nn.sigmoid(gate_pre)
    hidden = lax.reduce_precision(gate_pre * sigma * up_pre, 8, 7)
    scale = gate[:, :, None]
    scaled = (scale * hidden).astype(jnp.bfloat16).reshape(rows, local_experts * ff)
    dg = jnp.sum(hidden * d_raw, axis=2)
    dg_part = jnp.sum(dg[:, None, :] * hit, axis=2)
    d_hidden = scale * d_raw
    d_gate = d_hidden * up_pre * sigma * (1.0 + gate_pre * (1.0 - sigma))
    d_up = d_hidden * gate_pre * sigma
    d_pre = jnp.stack([d_gate, d_up], axis=2).astype(jnp.bfloat16).reshape(rows, -1)
    mixed_part = dot(scaled, w_down, ((1,), (0,)))
    dx_part = dot(d_pre, w_both, ((1,), (0,)))
    grad_out = dot(scaled, g, ((0,), (0,))).astype(jnp.bfloat16)
    grad_in = dot(d_pre, x, ((0,), (0,))).astype(jnp.bfloat16)
    pad = jnp.zeros((rows, 128 - 2 * top_k), jnp.bfloat16)
    sums = (mixed_part, dx_part, dg_part)
    for axis in ALL[::-1]:
        count = lax.axis_size(axis)
        mixed, d_tokens, d_gates = sums
        dg_top = lax.reduce_precision(d_gates, 8, 7)
        part = jnp.concatenate(
            [v.astype(jnp.bfloat16) for v in (mixed, d_tokens, dg_top, d_gates - dg_top)]
            + [pad[: d_gates.shape[0]]],
            axis=1,
        )
        part = part.reshape(count, -1, part.shape[1])
        got = lax.all_to_all(part, axis, split_axis=0, concat_axis=0, tiled=True)
        got = jnp.sum(got.astype(jnp.float32), axis=0)
        end = 2 * width
        d_gates = got[:, end : end + top_k] + got[:, end + top_k : end + 2 * top_k]
        sums = (got[:, :width], got[:, width:end], d_gates)
    mixed, d_tokens, d_gates = sums
    return (
        mixed.astype(jnp.bfloat16),
        d_tokens.astype(jnp.bfloat16),
        d_gates,
        grad_in.reshape(w_in.shape),
        grad_out.reshape(w_out.shape),
    )


def solution(mesh):
    return jax.shard_map(
        per_device,
        mesh=mesh,
        in_specs=(
            P(("dp", "expert", "tensor"), None),
            P(("dp", "expert", "tensor"), None),
            P(("dp", "expert", "tensor"), None),
            P(("dp", "expert", "tensor"), None),
            P("expert", None, ("dp", "tensor"), None),
            P("expert", ("dp", "tensor"), None),
        ),
        out_specs=(
            P(("dp", "expert", "tensor"), None),
            P(("dp", "expert", "tensor"), None),
            P(("dp", "expert", "tensor"), None),
            P("expert", None, ("dp", "tensor"), None),
            P("expert", ("dp", "tensor"), None),
        ),
        check_vma=False,
    )
```

time: 362 us -> 174 us (0.48)
  blocking collectives: 195 us -> 20.3 us
  waiting for transfers between devices: 63.3 us -> 41.3 us
  starting transfers between devices: 6.83 us -> 20.9 us
  between operations: 14.8 us -> 0.82 us
  local copies, waits for them, and re-layouts: 9.46 us -> 15.9 us
  matrix products: 71.5 us -> 66.3 us
  other arithmetic: 1.14 us -> 5.13 us
    unnamed x1 -> x0, blocking collectives: 183 us -> none
    all_gather x2 -> x0, waiting for transfers between devices: 60.7 us -> none  [the longest x1 32.3 us: per_device(): lax.all_gather(to_groups(got_x, owners, local_experts), ('dp', 'tensor'),...]
    all_to_all x2 -> x4, waiting for transfers between devices: 2.52 us -> 41.3 us  [the longest x1 25.2 us: spread(): return lax.all_to_all(copies, axis, split_axis=0, concat_axis=0, tiled=True)]
    all_to_all x2 -> x4, starting transfers between devices: 6.75 us -> 20.9 us  [the longest x3 12.5 us: per_device(): got = lax.all_to_all(part, axis, split_axis=0, concat_axis=0, tiled=True)]
    all_to_all x2, blocking collectives: 12.1 us -> 20.3 us  [spread(): return lax.all_to_all(copies, axis, split_axis=0, concat_axis=0, tiled=True)]
    concatenate x0 -> x3, local copies, waits for them, and re-layouts: none -> 5.61 us  [per_device(): jnp.concatenate([v.astype(jnp.bfloat16) for v in (mixed, d_tokens, dg_top...]
    dot_general x10 -> x6, matrix products: 71.5 us -> 66.3 us  [dot(): lax.dot_general(a, b, (dims, ((), ())), preferred_element_type=jnp.float32)]
  transfers between devices with their start and end apart: 4 -> 4, of which waited for: 3 -> 3; matrix products, arithmetic and copies ran while one was open for 8% -> 14% of each run, Pallas kernels for 0% -> 0%
where the time goes in v1:
time: 174 us; the launch traced here: 171 us
  matrix products  66.3 us (38%)
  waiting for transfers between devices  41.3 us (24%)
  starting transfers between devices  20.9 us (12%)
  blocking collectives  20.3 us (12%)
  local copies, waits for them, and re-layouts  15.9 us (9%)
  other arithmetic  5.13 us (3%)
    dot_general x6, matrix products, dot(): lax.dot_general(a, b, (dims, ((), ())), preferred_element_type=jnp.float32)  66.3 us
    all_to_all x1, waiting for transfers between devices, spread(): return lax.all_to_all(copies, axis, split_axis=0, concat_axis=0, tiled=True)  25.2 us
    all_to_all x2, blocking collectives, spread(): return lax.all_to_all(copies, axis, split_axis=0, concat_axis=0, tiled=True)  20.3 us
    all_to_all x3, waiting for transfers between devices, per_device(): got = lax.all_to_all(part, axis, split_axis=0, concat_axis=0, tiled=True)  16.2 us
    all_to_all x3, starting transfers between devices, per_device(): got = lax.all_to_all(part, axis, split_axis=0, concat_axis=0, tiled=True)  12.5 us
    all_to_all x1, starting transfers between devices, spread(): return lax.all_to_all(copies, axis, split_axis=0, concat_axis=0, tiled=True)  8.44 us
    concatenate x3, local copies, waits for them, and re-layouts, per_device(): jnp.concatenate([v.astype(jnp.bfloat16) for v in (mixed, d_tokens, dg_top...  5.61 us
    unnamed x10, local copies, waits for them, and re-layouts  3.62 us
  transfers between devices with their start and end apart: 4, of which 3 were waited for; matrix products, arithmetic and copies ran while one was open for 14% of the time, Pallas kernels for 0%

profile of v1, /device:TPU:1, one launch (start us, length us, event | category | flops | bytes accessed | tf_op | source)
XLA Modules:
  0.0 170.7 jit_solution(7839693180587414223)
XLA Ops:
  0.6 0.8 copy.59
  1.4 0.8 copy.58
  2.3 0.8 pad_maximum_fusion
  3.1 12.4 %all_to_all.30 = bf16[4,4,8320]{2,1,0:T(4,128)(2,1)S(1)} all-to-all(bf16[4,4,8320]{2,1,0:T(4,128)(2,1)S(1)} %broadcast_in_dim.8), channel_id=1, replica_groups=mesh['dp'=4,'expert'=2,'tensor'=4] {'dp'}, dimensions={0} | all-to-all | bytes 532480 | tf_op jit(solution)/shard_map/all_to_all | solution.py:21
  15.6 0.1 broadcast_in_dim.9
  15.7 7.9 %all_to_all.31 = bf16[2,4,4,8320]{3,2,1,0:T(4,128)(2,1)S(1)} all-to-all(bf16[2,4,4,8320]{3,2,1,0:T(4,128)(2,1)S(1)} %broadcast_in_dim.9), channel_id=1, replica_groups=mesh['dp'=4,'expert'=2,'tensor'=4] {'expert'}, dimensions={0} | all-to-all | bytes 1064960 | tf_op jit(solution)/shard_map/all_to_all | solution.py:21
  23.6 1.9 %broadcast_in_dim.10 = bf16[4,2,4,4,8320]{4,3,2,1,0:T(4,128)(2,1)} broadcast(bf16[2,4,4,8320]{3,2,1,0:T(4,128)(2,1)S(1)} %all_to_all.31), dimensions={1,2,3,4} | broadcast | bytes 2662400 | tf_op jit(solution)/shard_map/broadcast_in_dim | solution.py:20
  25.5 8.4 %all-to-all-start.2 = ((bf16[4,2,4,4,8320]{4,3,2,1,0:T(4,128)(2,1)}), bf16[4,2,4,4,8320]{4,3,2,1,0:T(4,128)(2,1)}, u32[]{:S(2)}, u32[]{:S(2)}) async-start(bf16[4,2,4,4,8320]{4,3,2,1,0:T(4,128)(2,1)} %broadcast_in_dim.10), calls=%async_computation.2 | async-start | bytes 4259840 | tf_op jit(solution)/shard_map/all_to_all | solution.py:21
  33.9 25.2 %all-to-all-done.2 = bf16[4,2,4,4,8320]{4,3,2,1,0:T(4,128)(2,1)} async-done(((bf16[4,2,4,4,8320]{4,3,2,1,0:T(4,128)(2,1)}), bf16[4,2,4,4,8320]{4,3,2,1,0:T(4,128)(2,1)}, u32[]{:S(2)}, u32[]{:S(2)}) %all-to-all-start.2) | async-done | bytes 2129952 | tf_op jit(solution)/shard_map/all_to_all | solution.py:21
  59.1 2.5 %reshape.54 = bf16[128,8320]{1,0:T(8,128)(2,1)S(1)} reshape(bf16[4,2,4,4,8320]{4,3,2,1,0:T(4,128)(2,1)} %all-to-all-done.2) | data formatting | bytes 4259840 | tf_op jit(solution)/shard_map/reshape | solution.py:35
  61.7 1.3 copy-done
  63.0 13.7 %fusion.2 = f32[128,4,2,448]{0,3,2,1:T(8,128)S(1)} fusion(bf16[4,2,448,4096]{3,2,1,0:T(8,128)(2,1)} %param.10, bf16[128,8320]{1,0:T(8,128)(2,1)} %copy-done), kind=kOutput, calls=%fused_computation.10 | convolution fusion | flops 3758096384 | bytes 32243712 | tf_op jit(solution)/shard_map/dot_general | solution.py:10
  76.8 7.8 %multiply_reduce_fusion = (f32[128,4]{0,1:T(4,128)S(1)}, f32[128,4,448]{0,2,1:T(8,128)S(1)}) fusion(f32[128,4,2,448]{0,3,2,1:T(8,128)S(1)} %fusion.2, bf16[4,448,4096]{2,1,0:T(8,128)(2,1)} %param.11, bf16[128,8320]{1,0:T(8,128)(2,1)} %copy-done), kind=kOutput, calls=%fused_computation.42 | convolution fusion | flops 1880882688 | bytes 18483200 | tf_op jit(solution)/shard_map/dot_general | solution.py:10
  84.7 8.3 %fusion = bf16[128,4096]{1,0:T(8,128)(2,1)} fusion(bf16[4,448,4096]{2,1,0:T(8,128)(2,1)} %param.11, f32[128,4]{0,1:T(4,128)S(1)} %get-tuple-element.36, f32[128,4,2,448]{0,3,2,1:T(8,128)S(1)} %fusion.2), kind=kOutput, calls=%fused_computation.4 | convolution fusion | flops 1881407488 | bytes 17565696 | tf_op jit(solution)/shard_map/dot_general | solution.py:10
  93.0 1.2 fusion.23
  94.2 0.1 copy.64
  94.4 0.1 copy.65
  94.5 13.5 %fusion.1 = bf16[128,4096]{1,0:T(8,128)(2,1)S(1)} fusion(bf16[4,2,448,4096]{3,2,1,0:T(8,128)(2,1)} %param.10, bf16[128,4,1,448]{0,3,1,2:T(8,128)(2,1)} %get-tuple-element.38, bf16[128,4,1,448]{0,3,1,2:T(8,128)(2,1)S(1)} %get-tuple-element.37), kind=kOutput, calls=%fused_computation.5 | convolution fusion | flops 3759079424 | bytes 31326208 | tf_op jit(solution)/shard_map/dot_general | solution.py:10
  108.0 4.6 %concatenate.18 = bf16[128,8320]{1,0:T(8,128)(2,1)} concatenate(bf16[128,4096]{1,0:T(8,128)(2,1)} %fusion, bf16[128,4096]{1,0:T(8,128)(2,1)S(1)} %fusion.1, bf16[128,2]{1,0:T(8,128)(2,1)S(1)} %copy.64, bf16[128,2]{1,0:T(8,128)(2,1)S(1)} %copy.65, bf16[128,124]{1,0:T(8,128)(2,1)S(1)} %broadcast_in_dim.11), dimensions={1} | concatenate | bytes 4259840 | tf_op jit(solution)/shard_map/concatenate | solution.py:73
  112.6 5.5 %all-to-all-start.3 = ((bf16[4,32,8320]{2,1,0:T(8,128)(2,1)}), bf16[4,32,8320]{2,1,0:T(8,128)(2,1)}, u32[]{:S(2)}, u32[]{:S(2)}) async-start(bf16[4,32,8320]{2,1,0:T(8,128)(2,1)} %bitcast.115), calls=%async_computation.3 | async-start | bytes 4259840 | tf_op jit(solution)/shard_map/all_to_all | solution.py:79
  118.3 15.5 %convolution_convert_fusion = bf16[3584,4096]{1,0:T(8,128)(2,1)} fusion(bf16[128,3584]{0,1:T(8,128)(2,1)S(1)} %bitcast.116, bf16[128,8320]{1,0:T(8,128)(2,1)} %copy-done), kind=kOutput, calls=%fused_computation | convolution fusion | flops 3772776448 | bytes 31326208 | tf_op jit(solution)/shard_map/dot_general | solution.py:10
  133.8 9.5 %all-to-all-done.3 = bf16[4,32,8320]{2,1,0:T(8,128)(2,1)} async-done(((bf16[4,32,8320]{2,1,0:T(8,128)(2,1)}), bf16[4,32,8320]{2,1,0:T(8,128)(2,1)}, u32[]{:S(2)}, u32[]{:S(2)}) %all-to-all-start.3) | async-done | bytes 2129952 | tf_op jit(solution)/shard_map/all_to_all | solution.py:79
  143.3 2.0 %convert_reduce_fusion = f32[32,8320]{1,0:T(8,128)S(1)} fusion(bf16[4,32,8320]{2,1,0:T(8,128)(2,1)} %all-to-all-done.3), kind=kLoop, calls=%fused_computation.6 | loop fusion | flops 1863680 | bytes 3194880 | tf_op jit(solution)/shard_map/reduce_sum | solution.py:80
  145.4 0.9 concatenate.19
  146.4 3.5 %all-to-all-start.4 = ((bf16[2,16,8320]{2,1,0:T(8,128)(2,1)}), bf16[2,16,8320]{2,1,0:T(8,128)(2,1)S(1)}, u32[]{:S(2)}, u32[]{:S(2)}) async-start(bf16[2,16,8320]{2,1,0:T(8,128)(2,1)} %bitcast.11), calls=%async_computation.4 | async-start | bytes 1064960 | tf_op jit(solution)/shard_map/all_to_all | solution.py:79
  150.0 0.3 fusion.27
  150.4 6.7 %all-to-all-done.4 = bf16[2,16,8320]{2,1,0:T(8,128)(2,1)S(1)} async-done(((bf16[2,16,8320]{2,1,0:T(8,128)(2,1)}), bf16[2,16,8320]{2,1,0:T(8,128)(2,1)S(1)}, u32[]{:S(2)}, u32[]{:S(2)}) %all-to-all-start.4) | async-done | bytes 532512 | tf_op jit(solution)/shard_map/all_to_all | solution.py:79
  157.3 0.8 reshape.57
  158.1 3.5 %all-to-all-start.5 = ((bf16[4,4,8320]{2,1,0:T(4,128)(2,1)}), bf16[4,4,8320]{2,1,0:T(4,128)(2,1)S(1)}, u32[]{:S(2)}, u32[]{:S(2)}) async-start(bf16[4,4,8320]{2,1,0:T(4,128)(2,1)} %reshape.57), calls=%async_computation.5 | async-start | bytes 532480 | tf_op jit(solution)/shard_map/all_to_all | solution.py:79
  161.6 7.5 %convolution_convert_fusion.1 = bf16[1792,4096]{1,0:T(8,128)(2,1)} fusion(bf16[128,1792]{0,1:T(8,128)(2,1)S(1)} %fusion.27, bf16[128,8320]{1,0:T(8,128)(2,1)S(1)} %copy-done.1), kind=kOutput, calls=%fused_computation.1 | convolution fusion | flops 1886388224 | bytes 16187392 | tf_op jit(solution)/shard_map/dot_general | solution.py:10
  169.4 0.6 fusion.45
  170.0 0.6 copy.67
  (33 shorter events, 1.3 us)
Async XLA Ops:
  25.5 33.6 %all-to-all-start.2 = ((bf16[4,2,4,4,8320]{4,3,2,1,0:T(4,128)(2,1)}), bf16[4,2,4,4,8320]{4,3,2,1,0:T(4,128)(2,1)}, u32[]{:S(2)}, u32[]{:S(2)}) async-start(bf16[4,2,4,4,8320]{4,3,2,1,0:T(4,128)(2,1)} %broadcast_in_dim.10), calls=%async_computation.2 | async-start | bytes 4259840 | tf_op jit(solution)/shard_map/all_to_all | solution.py:21
  61.6 1.3 copy-start
  63.0 13.7 %slice-start = ((bf16[128,8320]{1,0:T(8,128)(2,1)}), bf16[128,128]{1,0:T(8,128)(2,1)S(1)}, s32[]{:S(2)}) async-start(bf16[128,8320]{1,0:T(8,128)(2,1)} %copy-done), calls=%async_computation.6 | async-start | bytes 65536 | tf_op jit(solution)/shard_map/slice | solution.py:38
  112.6 5.5 %copy-start.2 = (bf16[128,4,1,448]{0,3,1,2:T(8,128)(2,1)S(1)}, bf16[128,4,1,448]{0,3,1,2:T(8,128)(2,1)}, u32[]{:S(2)}) copy-start(bf16[128,4,1,448]{0,3,1,2:T(8,128)(2,1)} %get-tuple-element.38) | copy-start | bytes 1376260
  112.6 30.6 %all-to-all-start.3 = ((bf16[4,32,8320]{2,1,0:T(8,128)(2,1)}), bf16[4,32,8320]{2,1,0:T(8,128)(2,1)}, u32[]{:S(2)}, u32[]{:S(2)}) async-start(bf16[4,32,8320]{2,1,0:T(8,128)(2,1)} %bitcast.115), calls=%async_computation.3 | async-start | bytes 4259840 | tf_op jit(solution)/shard_map/all_to_all | solution.py:79
  146.4 10.7 %all-to-all-start.4 = ((bf16[2,16,8320]{2,1,0:T(8,128)(2,1)}), bf16[2,16,8320]{2,1,0:T(8,128)(2,1)S(1)}, u32[]{:S(2)}, u32[]{:S(2)}) async-start(bf16[2,16,8320]{2,1,0:T(8,128)(2,1)} %bitcast.11), calls=%async_computation.4 | async-start | bytes 1064960 | tf_op jit(solution)/shard_map/all_to_all | solution.py:79
  150.3 11.3 %copy-start.1 = (bf16[128,8320]{1,0:T(8,128)(2,1)S(1)}, bf16[128,8320]{1,0:T(8,128)(2,1)}, u32[]{:S(2)}) copy-start(bf16[128,8320]{1,0:T(8,128)(2,1)} %copy-done) | copy-start | bytes 6389764
  158.1 11.0 %all-to-all-start.5 = ((bf16[4,4,8320]{2,1,0:T(4,128)(2,1)}), bf16[4,4,8320]{2,1,0:T(4,128)(2,1)S(1)}, u32[]{:S(2)}, u32[]{:S(2)}) async-start(bf16[4,4,8320]{2,1,0:T(4,128)(2,1)} %reshape.57), calls=%async_computation.5 | async-start | bytes 532480 | tf_op jit(solution)/shard_map/all_to_all | solution.py:79
